TPU v7x, 32 devices: a whole 2x2x4 slice. The times are simulated.
32 devices in a mesh: rep: 2 (over x), fsdp: 4 (over z), ctx: 4 (over y, core).
Axes of the slice: x: 2, y: 2, z: 4, core: 2. Of those that a mesh axis runs over, the one named last changes fastest.
Arguments:
- inputs: bfloat16 [8, 1024, 2048], P(('rep', 'fsdp'), 'ctx'), may hold values from -6 to 6
- prefix: int32 [8], P(('rep', 'fsdp')), may hold values from 102 to 512
- joined_weight: bfloat16 [2048, 6144], P(('fsdp', 'ctx')), may hold values from -0.125 to 0.125
- query_bias: bfloat16 [2048], P(('fsdp', 'ctx')), may hold values from -3 to 3
- value_bias: bfloat16 [2048], P(('fsdp', 'ctx')), may hold values from -3 to 3
- dense_weight: bfloat16 [2048, 2048], P(('fsdp', 'ctx')), may hold values from -0.5 to 0.5
- dense_bias: bfloat16 [2048], P(('fsdp', 'ctx')), may hold values from -2 to 2
- expand_weight: bfloat16 [2048, 8192], P(('fsdp', 'ctx')), may hold values from -0.125 to 0.125
- expand_bias: bfloat16 [8192], P(('fsdp', 'ctx')), may hold values from -3 to 3
- shrink_weight: bfloat16 [8192, 2048], P(('fsdp', 'ctx')), may hold values from -0.0625 to 0.0625
- shrink_bias: bfloat16 [2048], P(('fsdp', 'ctx')), may hold values from -2 to 2
- first_gain: bfloat16 [2048], P(('fsdp', 'ctx')), may hold values from 0.5 to 1.5
- first_shift: bfloat16 [2048], P(('fsdp', 'ctx')), may hold values from -2 to 2
- second_gain: bfloat16 [2048], P(('fsdp', 'ctx')), may hold values from 0.5 to 1.5
- second_shift: bfloat16 [2048], P(('fsdp', 'ctx')), may hold values from -2 to 2
- cotangent: bfloat16 [8, 1024, 2048], P(('rep', 'fsdp'), 'ctx'), may hold values from -6 to 6
Outputs:
- layer_output: float32 [8, 1024, 2048], P(('rep', 'fsdp'), 'ctx')
- input_gradient: float32 [8, 1024, 2048], P(('rep', 'fsdp'), 'ctx')
- joined_gradient: float32 [2048, 6144], P(('fsdp', 'ctx'))
- query_bias_gradient: float32 [2048], P(('fsdp', 'ctx'))
- value_bias_gradient: float32 [2048], P(('fsdp', 'ctx'))
- dense_gradient: float32 [2048, 2048], P(('fsdp', 'ctx'))
- dense_bias_gradient: float32 [2048], P(('fsdp', 'ctx'))
- expand_gradient: float32 [2048, 8192], P(('fsdp', 'ctx'))
- expand_bias_gradient: float32 [8192], P(('fsdp', 'ctx'))
- shrink_gradient: float32 [8192, 2048], P(('fsdp', 'ctx'))
- shrink_bias_gradient: float32 [2048], P(('fsdp', 'ctx'))
- first_gain_gradient: float32 [2048], P(('fsdp', 'ctx'))
- first_shift_gradient: float32 [2048], P(('fsdp', 'ctx'))
- second_gain_gradient: float32 [2048], P(('fsdp', 'ctx'))
- second_shift_gradient: float32 [2048], P(('fsdp', 'ctx'))
All inputs are finite; a program needn't handle non-finite values.
Results may differ from a plain program's by a relative error of at most 0.014.
Values may be sent and summed in bfloat16 or wider, within the bound.
No kernel may reach another device: no remote copies, remote signals or barrier semaphores. Data moves between devices by JAX's collectives and lax.ppermute only.
A program may use at most 576 MiB of HBM per device.

v0:
```python
import jax
import jax.numpy as jnp
from jax import lax
from jax.sharding import PartitionSpec as P

H = 32
HD = 64


def layer_norm(values, gain, shift):
    average = jnp.mean(values, axis=-1, keepdims=True)
    centred = values - average
    variance = jnp.mean(centred * centred, axis=-1, keepdims=True)
    return centred * lax.rsqrt(variance + 1e-05) * gain + shift


def exact_gelu(values):
    return jax.nn.gelu(values, approximate=False)


def score_logits(query_heads, key_heads, prefix, first_place):
    raw = jnp.einsum("sqhe,skhe->shqk", query_heads, key_heads, preferred_element_type=jnp.float32)
    queries_here = query_heads.shape[1]
    length = key_heads.shape[1]
    heads = query_heads.shape[2]
    query_place = first_place + jnp.arange(queries_here, dtype=jnp.int32)
    key_place = jnp.arange(length, dtype=jnp.int32)
    distance = jnp.abs(query_place[:, None] - key_place[None, :]).astype(jnp.float32)
    allowed = (key_place[None, None, :] <= query_place[None, :, None]) | (
        key_place[None, None, :] < prefix[:, None, None]
    )
    order = jnp.arange(heads, dtype=jnp.int32).astype(jnp.float32)
    slopes = jnp.exp2(-8.0 * (order + 1.0) / heads)
    logits = raw * 0.125 - slopes[None, :, None, None] * distance[None, None]
    return (logits, allowed[:, None])


def shards(
    inputs,
    prefix,
    joined_weight,
    query_bias,
    value_bias,
    dense_weight,
    dense_bias,
    expand_weight,
    expand_bias,
    shrink_weight,
    shrink_bias,
    first_gain,
    first_shift,
    second_gain,
    second_shift,
    cotangent,
):
    sequences, span_rows, features = inputs.shape
    tokens = sequences * span_rows
    attn_parts = (
        lax.all_gather(joined_weight, ("fsdp", "ctx"), axis=0, tiled=True),
        lax.all_gather(query_bias, ("fsdp", "ctx"), axis=0, tiled=True),
        lax.all_gather(value_bias, ("fsdp", "ctx"), axis=0, tiled=True),
        lax.all_gather(dense_weight, ("fsdp", "ctx"), axis=0, tiled=True),
        lax.all_gather(dense_bias, ("fsdp", "ctx"), axis=0, tiled=True),
        lax.all_gather(first_gain, ("fsdp", "ctx"), axis=0, tiled=True),
        lax.all_gather(first_shift, ("fsdp", "ctx"), axis=0, tiled=True),
    )
    joined_all, qbias_all, vbias_all, dense_all, dbias_all, gain_one, shift_one = attn_parts
    start = inputs.astype(jnp.float32).reshape(tokens, features)
    gain_first = gain_one.astype(jnp.float32)
    shift_first = shift_one.astype(jnp.float32)
    normed = layer_norm(start, gain_first, shift_first).astype(jnp.bfloat16)
    projected = jnp.dot(normed, joined_all, preferred_element_type=jnp.float32)
    queries = (projected[:, :features] + qbias_all.astype(jnp.float32)).astype(jnp.bfloat16)
    keys_own = projected[:, features : 2 * features].astype(jnp.bfloat16)
    values_own = (projected[:, 2 * features :] + vbias_all.astype(jnp.float32)).astype(jnp.bfloat16)
    keys_all, values_all = (
        lax.all_gather(keys_own.reshape(sequences, span_rows, features), "ctx", axis=1, tiled=True),
        lax.all_gather(
            values_own.reshape(sequences, span_rows, features), "ctx", axis=1, tiled=True
        ),
    )
    length = keys_all.shape[1]
    query_heads = queries.reshape(sequences, span_rows, H, HD)
    key_heads = keys_all.reshape(sequences, length, H, HD)
    value_heads = values_all.reshape(sequences, length, H, HD)
    first_place = lax.axis_index("ctx") * span_rows
    logits, allowed = score_logits(query_heads, key_heads, prefix, first_place)
    masked = jnp.where(allowed, logits, -1e30)
    largest = jnp.max(masked, axis=-1, keepdims=True)
    exponent = jnp.exp(masked - largest)
    totals = jnp.sum(exponent, axis=-1, keepdims=True)
    log_total = largest + jnp.log(totals)
    probs_low = (exponent / totals).astype(jnp.bfloat16)
    mixture = jnp.einsum(
        "shqk,skhe->sqhe", probs_low, value_heads, preferred_element_type=jnp.float32
    )
    attended = mixture.reshape(tokens, features).astype(jnp.bfloat16)
    midway = (
        start
        + jnp.dot(attended, dense_all, preferred_element_type=jnp.float32)
        + dbias_all.astype(jnp.float32)
    )
    mlp_parts = (
        lax.all_gather(expand_weight, ("fsdp", "ctx"), axis=0, tiled=True),
        lax.all_gather(expand_bias, ("fsdp", "ctx"), axis=0, tiled=True),
        lax.all_gather(shrink_weight, ("fsdp", "ctx"), axis=0, tiled=True),
        lax.all_gather(shrink_bias, ("fsdp", "ctx"), axis=0, tiled=True),
        lax.all_gather(second_gain, ("fsdp", "ctx"), axis=0, tiled=True),
        lax.all_gather(second_shift, ("fsdp", "ctx"), axis=0, tiled=True),
    )
    expand_all, ebias_all, shrink_all, sbias_all, gain_two, shift_two = mlp_parts
    gain_second = gain_two.astype(jnp.float32)
    shift_second = shift_two.astype(jnp.float32)
    normed_two = layer_norm(midway, gain_second, shift_second).astype(jnp.bfloat16)
    expanded = jnp.dot(
        normed_two, expand_all, preferred_element_type=jnp.float32
    ) + ebias_all.astype(jnp.float32)
    activated = exact_gelu(expanded).astype(jnp.bfloat16)
    result = (
        midway
        + jnp.dot(activated, shrink_all, preferred_element_type=jnp.float32)
        + sbias_all.astype(jnp.float32)
    )
    again_mlp = (
        lax.all_gather(expand_weight, ("fsdp", "ctx"), axis=0, tiled=True),
        lax.all_gather(shrink_weight, ("fsdp", "ctx"), axis=0, tiled=True),
        lax.all_gather(second_gain, ("fsdp", "ctx"), axis=0, tiled=True),
    )
    back_expand, back_shrink = (again_mlp[0], again_mlp[1])
    back_gain_two = again_mlp[2].astype(jnp.float32)
    grad_out = cotangent.reshape(tokens, features)
    grad_out_float = grad_out.astype(jnp.float32)
    shrink_term = jnp.einsum("rf,rd->fd", activated, grad_out, preferred_element_type=jnp.float32)
    sbias_term = jnp.sum(grad_out_float, axis=0)
    d_activated = jnp.einsum("rd,fd->rf", grad_out, back_shrink, preferred_element_type=jnp.float32)
    d_expanded = jax.vjp(exact_gelu, expanded)[1](d_activated)[0].astype(jnp.bfloat16)
    expand_term = jnp.einsum(
        "rd,rf->df", normed_two, d_expanded, preferred_element_type=jnp.float32
    )
    ebias_term = jnp.sum(d_expanded.astype(jnp.float32), axis=0)
    d_normed_two = jnp.einsum(
        "rf,df->rd", d_expanded, back_expand, preferred_element_type=jnp.float32
    )
    norm_back_two = jax.vjp(layer_norm, midway, back_gain_two, shift_second)[1]
    d_mid_norm, gain_two_term, shift_two_term = norm_back_two(d_normed_two)
    d_midway = grad_out_float + d_mid_norm
    mlp_grads = (
        lax.psum_scatter(expand_term, ("fsdp", "ctx"), scatter_dimension=0, tiled=True),
        lax.psum_scatter(ebias_term, ("fsdp", "ctx"), scatter_dimension=0, tiled=True),
        lax.psum_scatter(shrink_term, ("fsdp", "ctx"), scatter_dimension=0, tiled=True),
        lax.psum_scatter(sbias_term, ("fsdp", "ctx"), scatter_dimension=0, tiled=True),
        lax.psum_scatter(gain_two_term, ("fsdp", "ctx"), scatter_dimension=0, tiled=True),
        lax.psum_scatter(shift_two_term, ("fsdp", "ctx"), scatter_dimension=0, tiled=True),
    )
    again_attn = (
        lax.all_gather(joined_weight, ("fsdp", "ctx"), axis=0, tiled=True),
        lax.all_gather(dense_weight, ("fsdp", "ctx"), axis=0, tiled=True),
        lax.all_gather(first_gain, ("fsdp", "ctx"), axis=0, tiled=True),
    )
    back_joined, back_dense = (again_attn[0], again_attn[1])
    back_gain_one = again_attn[2].astype(jnp.float32)
    d_attended_out = d_midway.astype(jnp.bfloat16)
    dense_term = jnp.einsum(
        "rd,re->de", attended, d_attended_out, preferred_element_type=jnp.float32
    )
    dbias_term = jnp.sum(d_attended_out.astype(jnp.float32), axis=0)
    d_attended = jnp.einsum(
        "re,de->rd", d_attended_out, back_dense, preferred_element_type=jnp.float32
    ).astype(jnp.bfloat16)
    d_heads = d_attended.reshape(sequences, span_rows, H, HD)
    logits_again, allowed_again = score_logits(query_heads, key_heads, prefix, first_place)
    probs = jnp.where(allowed_again, jnp.exp(logits_again - log_total), 0.0)
    probs_again = probs.astype(jnp.bfloat16)
    d_probs = jnp.einsum(
        "sqhe,skhe->shqk", d_heads, value_heads, preferred_element_type=jnp.float32
    )
    weighted = jnp.sum(probs * d_probs, axis=-1, keepdims=True)
    d_raw = (probs * (d_probs - weighted) * 0.125).astype(jnp.bfloat16)
    d_queries = jnp.einsum("shqk,skhe->sqhe", d_raw, key_heads, preferred_element_type=jnp.float32)
    d_keys_full = jnp.einsum(
        "shqk,sqhe->skhe", d_raw, query_heads, preferred_element_type=jnp.float32
    )
    d_values_full = jnp.einsum(
        "shqk,sqhe->skhe", probs_again, d_heads, preferred_element_type=jnp.float32
    )
    d_keys, d_values = (
        lax.psum_scatter(
            d_keys_full.reshape(sequences, length, features).astype(jnp.bfloat16),
            "ctx",
            scatter_dimension=1,
            tiled=True,
        ).astype(jnp.float32),
        lax.psum_scatter(
            d_values_full.reshape(sequences, length, features).astype(jnp.bfloat16),
            "ctx",
            scatter_dimension=1,
            tiled=True,
        ).astype(jnp.float32),
    )
    d_queries_low = d_queries.reshape(tokens, features).astype(jnp.bfloat16)
    d_keys_low = d_keys.reshape(tokens, features).astype(jnp.bfloat16)
    d_values_low = d_values.reshape(tokens, features).astype(jnp.bfloat16)
    qbias_term = jnp.sum(d_queries_low.astype(jnp.float32), axis=0)
    vbias_term = jnp.sum(d_values_low.astype(jnp.float32), axis=0)
    d_projected = jnp.concatenate([d_queries_low, d_keys_low, d_values_low], axis=1)
    joined_term = jnp.einsum("rd,re->de", normed, d_projected, preferred_element_type=jnp.float32)
    d_normed = jnp.einsum("re,de->rd", d_projected, back_joined, preferred_element_type=jnp.float32)
    norm_back_one = jax.vjp(layer_norm, start, back_gain_one, shift_first)[1]
    d_start_norm, gain_one_term, shift_one_term = norm_back_one(d_normed)
    input_gradient = d_midway + d_start_norm
    attn_grads = (
        lax.psum_scatter(joined_term, ("fsdp", "ctx"), scatter_dimension=0, tiled=True),
        lax.psum_scatter(qbias_term, ("fsdp", "ctx"), scatter_dimension=0, tiled=True),
        lax.psum_scatter(vbias_term, ("fsdp", "ctx"), scatter_dimension=0, tiled=True),
        lax.psum_scatter(dense_term, ("fsdp", "ctx"), scatter_dimension=0, tiled=True),
        lax.psum_scatter(dbias_term, ("fsdp", "ctx"), scatter_dimension=0, tiled=True),
        lax.psum_scatter(gain_one_term, ("fsdp", "ctx"), scatter_dimension=0, tiled=True),
        lax.psum_scatter(shift_one_term, ("fsdp", "ctx"), scatter_dimension=0, tiled=True),
    )
    summed = (
        lax.psum(attn_grads[0].astype(jnp.bfloat16), "rep").astype(jnp.float32),
        lax.psum(attn_grads[1].astype(jnp.bfloat16), "rep").astype(jnp.float32),
        lax.psum(attn_grads[2].astype(jnp.bfloat16), "rep").astype(jnp.float32),
        lax.psum(attn_grads[3].astype(jnp.bfloat16), "rep").astype(jnp.float32),
        lax.psum(attn_grads[4].astype(jnp.bfloat16), "rep").astype(jnp.float32),
        lax.psum(attn_grads[5].astype(jnp.bfloat16), "rep").astype(jnp.float32),
        lax.psum(attn_grads[6].astype(jnp.bfloat16), "rep").astype(jnp.float32),
        lax.psum(mlp_grads[0].astype(jnp.bfloat16), "rep").astype(jnp.float32),
        lax.psum(mlp_grads[1].astype(jnp.bfloat16), "rep").astype(jnp.float32),
        lax.psum(mlp_grads[2].astype(jnp.bfloat16), "rep").astype(jnp.float32),
        lax.psum(mlp_grads[3].astype(jnp.bfloat16), "rep").astype(jnp.float32),
        lax.psum(mlp_grads[4].astype(jnp.bfloat16), "rep").astype(jnp.float32),
        lax.psum(mlp_grads[5].astype(jnp.bfloat16), "rep").astype(jnp.float32),
    )
    attn_grads = summed[:7]
    mlp_grads = summed[7:]
    return (
        result.reshape(sequences, span_rows, features),
        input_gradient.reshape(sequences, span_rows, features),
        attn_grads[0],
        attn_grads[1],
        attn_grads[2],
        attn_grads[3],
        attn_grads[4],
        mlp_grads[0],
        mlp_grads[1],
        mlp_grads[2],
        mlp_grads[3],
        attn_grads[5],
        attn_grads[6],
        mlp_grads[4],
        mlp_grads[5],
    )


def solution(mesh):
    in_specs = (
        P(("rep", "fsdp"), "ctx", None),
        P(("rep", "fsdp")),
        P(("fsdp", "ctx"), None),
        P(("fsdp", "ctx")),
        P(("fsdp", "ctx")),
        P(("fsdp", "ctx"), None),
        P(("fsdp", "ctx")),
        P(("fsdp", "ctx"), None),
        P(("fsdp", "ctx")),
        P(("fsdp", "ctx"), None),
        P(("fsdp", "ctx")),
        P(("fsdp", "ctx")),
        P(("fsdp", "ctx")),
        P(("fsdp", "ctx")),
        P(("fsdp", "ctx")),
        P(("rep", "fsdp"), "ctx", None),
    )
    out_specs = (
        P(("rep", "fsdp"), "ctx", None),
        P(("rep", "fsdp"), "ctx", None),
        P(("fsdp", "ctx"), None),
        P(("fsdp", "ctx")),
        P(("fsdp", "ctx")),
        P(("fsdp", "ctx"), None),
        P(("fsdp", "ctx")),
        P(("fsdp", "ctx"), None),
        P(("fsdp", "ctx")),
        P(("fsdp", "ctx"), None),
        P(("fsdp", "ctx")),
        P(("fsdp", "ctx")),
        P(("fsdp", "ctx")),
        P(("fsdp", "ctx")),
        P(("fsdp", "ctx")),
    )
    return jax.shard_map(shards, mesh=mesh, in_specs=in_specs, out_specs=out_specs, check_vma=False)
```

profile of v0, /device:TPU:0, one launch (start us, length us, event | category | flops | bytes accessed | tf_op | source)
XLA Modules:
  0.0 2958.1 jit_solution(15318190174671491095)
XLA Ops:
  8.0 23.2 all-gather.5
  31.2 17.5 all-gather.4
  48.7 18.9 all-gather.2
  67.6 17.5 all-gather.3
  88.3 52.7 %all-gather.18.cloned.1.call-done = bf16[2048,6144]{1,0:T(8,128)(2,1)} async-done(((bf16[128,6144]{1,0:T(8,128)(2,1)}), bf16[2048,6144]{1,0:T(8,128)(2,1)}) %all-gather.18.cloned.1.call-update) | async-done | bytes 25165840 | tf_op jit(solution)/shard_map/all_gather | solution.py:59
  141.0 12.1 fusion.78
  153.2 2.6 copy-done.9
  157.4 2.7 slice.23
  162.6 20.3 all-gather.6
  182.9 17.3 all-gather.7
  200.3 18.7 all-gather.8
  219.0 17.9 all-gather.9
  238.7 6.8 copy.43
  245.5 6.4 copy.45
  251.9 18.6 select_reduce_fusion
  270.5 15.0 fusion.2
  285.5 15.1 fusion.54
  300.6 5.5 all-gather.20.cloned.1.call-done
  306.1 6.2 fusion.85
  312.7 161.2 %all-gather.22.cloned.1.call-done = bf16[2048,8192]{1,0:T(8,128)(2,1)} async-done(((bf16[128,8192]{1,0:T(8,128)(2,1)}), bf16[2048,8192]{1,0:T(8,128)(2,1)}) %all-gather.22.cloned.1.call-update) | async-done | bytes 33554448 | tf_op jit(solution)/shard_map/all_gather | solution.py:104
  473.8 20.0 convolution_add_fusion
  493.8 149.6 %all-gather.24.cloned.1.call-done = bf16[8192,2048]{1,0:T(8,128)(2,1)} async-done(((bf16[512,2048]{1,0:T(8,128)(2,1)}), bf16[8192,2048]{1,0:T(8,128)(2,1)}) %all-gather.24.cloned.1.call-update) | async-done | bytes 33554448 | tf_op jit(solution)/shard_map/all_gather | solution.py:106
  643.4 33.6 %convert_reduce_fusion = (f32[8192]{0:T(1024)}, bf16[256,8192]{1,0:T(8,128)(2,1)}) fusion(f32[256,8192]{1,0:T(8,128)} %convolution_add_fusion, bf16[8192,2048]{1,0:T(8,128)(2,1)} %all-gather.24.cloned.1.call-done, bf16[1,256,2048]{2,1,0:T(8,128)(2,1)S(1)} %copy-done.10), kind=kOutput, calls=%fused_computation.24 | convolution fusion | flops 8745115648 | bytes 47218688 | tf_op jit(solution)/shard_map/rd,fd->rf/dot_general | solution.py:135
  677.0 18.4 multiply_reduce_fusion.1
  699.9 6.7 convolution_convert_fusion
  708.1 15.6 fusion.30
  723.8 17.2 fusion.88
  741.0 61.5 %fusion.27 = bf16[32,64,1024]{2,1,0:T(8,128)(2,1)} fusion(bf16[256,32,64]{0,2,1:T(8,128)(2,1)} %bitcast.141, f32[32,256,1024]{2,1,0:T(8,128)} %fusion.88, f32[32,256,1024]{2,1,0:T(8,128)} %get-tuple-element.53, f32[32,256]{1,0:T(8,128)S(1)} %log_add_fusion, pred[256,1024]{1,0:T(8,128)(4,1)S(1)} %fusion.64), kind=kOutput, calls=%fused_computation.43 | convolution fusion | flops 1151345664 | bytes 72646656 | tf_op jit(solution)/shard_map/shqk,sqhe->skhe/dot_general | solution.py:180
  802.5 9.7 fusion.89
  812.4 61.6 %convert_reduce_fusion.5 = (f32[32,64]{1,0:T(8,128)}, bf16[32,64,256]{2,1,0:T(8,128)(2,1)S(1)}) fusion(bf16[1024,32,64]{0,2,1:T(8,128)(2,1)} %bitcast.134, f32[32,256,1024]{2,1,0:T(8,128)} %fusion.88, f32[32,256,1024]{2,1,0:T(8,128)} %get-tuple-element.53, f32[32,256]{1,0:T(8,128)S(1)} %log_add_fusion, pred[256,1024]{1,0:T(8,128)(4,1)S(1)} %fusion.64), kind=kOutput, calls=%fused_computation.75 | convolution fusion | flops 1150819328 | bytes 72654848 | tf_op jit(solution)/shard_map/shqk,skhe->sqhe/dot_general | solution.py:179
  874.0 20.7 fusion.56
  894.8 34.3 %fusion.58 = f32[8192,2048]{1,0:T(8,128)} fusion(bf16[1,256,2048]{2,1,0:T(8,128)(2,1)S(1)} %copy-done.10, f32[256,8192]{1,0:T(8,128)} %convolution_add_fusion), kind=kOutput, calls=%fused_computation.85 | convolution fusion | flops 8726249472 | bytes 76546048 | tf_op jit(solution)/shard_map/rf,rd->fd/dot_general | solution.py:133
  930.8 26.1 fusion.81
  959.4 20.2 all-gather.10
  979.7 50.7 %reduce-scatter.13.cloned.1.call-done = f32[128,2048]{1,0:T(8,128)} async-done(((f32[2048,2048]{1,0:T(8,128)}), f32[128,2048]{1,0:T(8,128)}) %reduce-scatter.13.cloned.1.call-update) | async-done | bytes 1048592 | tf_op jit(solution)/shard_map/reduce_scatter | solution.py:215
  1032.5 468.8 %reduce-scatter.11.cloned.1.call-done = f32[128,6144]{1,0:T(8,128)} async-done(((f32[2048,6144]{1,0:T(8,128)}), f32[128,6144]{1,0:T(8,128)}) %reduce-scatter.11.cloned.1.call-update) | async-done | bytes 3145744 | tf_op jit(solution)/shard_map/reduce_scatter | solution.py:212
  1501.2 3.2 convert_element_type.300
  1504.5 637.2 %reduce-scatter.17.cloned.1.call-done = f32[512,2048]{1,0:T(8,128)} async-done(((f32[8192,2048]{1,0:T(8,128)}), f32[512,2048]{1,0:T(8,128)}) %reduce-scatter.17.cloned.1.call-update) | async-done | bytes 4194320 | tf_op jit(solution)/shard_map/reduce_scatter | solution.py:150
  2141.7 3.8 convert_element_type.318
  2145.5 636.3 %reduce-scatter.15.cloned.1.call-done = f32[128,8192]{1,0:T(8,128)} async-done(((f32[2048,8192]{1,0:T(8,128)}), f32[128,8192]{1,0:T(8,128)}) %reduce-scatter.15.cloned.1.call-update) | async-done | bytes 4194320 | tf_op jit(solution)/shard_map/reduce_scatter | solution.py:148
  2781.7 3.8 convert_element_type.313
  2785.6 31.8 %fusion.40 = f32[1,256,2048]{2,1,0:T(8,128)} fusion(f32[256,2048]{1,0:T(8,128)S(1)} %copy-done.4, bf16[8192,2048]{1,0:T(8,128)(2,1)} %all-gather.24.cloned.1.call-done, f32[2048]{0:T(1024)S(1)} %bitcast.159, f32[256,8192]{1,0:T(8,128)} %convolution_add_fusion), kind=kOutput, calls=%fused_computation.57 | convolution fusion | flops 8727298048 | bytes 46145536 | tf_op jit(solution)/shard_map/dot_general | solution.py:121
  2819.1 14.7 fusion.82
  2837.4 60.8 %all-reduce.9 = (bf16[2048]{0:T(1024)(128)(2,1)S(1)}, bf16[2048]{0:T(1024)(128)(2,1)S(1)}, bf16[2048]{0:T(1024)(128)(2,1)S(1)}, bf16[8192]{0:T(1024)(128)(2,1)S(...) all-reduce(f32[2048]{0:T(1024)S(1)} %reduce_sum.189, ...), channel_id=7, replica_groups=mesh['rep'=2,'fsdp'=4,'ctx'=4] {'fsdp','ctx'}, use_global_device_ids=true, to_apply=%region_16.17.clone | all-reduce | flops 24576 | bytes 147456
  2898.9 5.1 all-reduce.10
  2908.7 30.4 %all-reduce.14.cloned.1.call-done = (bf16[128,6144]{1,0:T(8,128)(2,1)}, bf16[128,2048]{1,0:T(8,128)(2,1)}, bf16[128,8192]{1,0:T(8,128)(2,1)}, bf16[512,2048]{1,0:T(8,128)(2,1)}) async-done(((bf16[128,6144]{1,0:T(8,128)(2,1)}, bf16[128,2048]{1,0:T(8,128)(2,1)}, bf16[128,8192]{1,0:T(8,128)(2,1)}, bf16[512,2048]{1,0:T(8,128)(2,1)}), (bf16[128,6144]{1,0:T(8,128)(2,1)}, bf16[128,2048]{1,0:T(8,128)(2,1)}, ...) | async-done | bytes 6291472 | tf_op jit(solution)/shard_map/psum | solution.py:221
  2941.4 3.4 convert_element_type.301
  2944.8 4.0 convert_element_type.314
  (185 shorter events, 36.0 us)
Async XLA Ops:
  7.2 133.9 %all-gather.18.cloned.1.call-start = ((), (), s32[]{:S(2)}) async-start(), calls=%async_computation.6 | async-start | bytes 26738688 | tf_op jit(solution)/shard_map/all_gather | solution.py:59
  7.9 230.8 %all-gather.26.cloned.1.call-start = ((), (), s32[]{:S(2)}) async-start(), calls=%async_computation.16 | async-start | bytes 5242880 | tf_op jit(solution)/shard_map/all_gather | solution.py:78
  67.6 85.6 %copy-start.15 = (f32[16,1,128]{2,1,0:T(1,128)}, f32[16,1,128]{2,1,0:T(1,128)S(1)}, u32[]{:S(2)}) copy-start(f32[16,1,128]{2,1,0:T(1,128)S(1)} %convert_element_type.330) | copy-start | bytes 24580
  85.1 68.0 %copy-start.18 = (f32[16,1,128]{2,1,0:T(1,128)}, f32[16,1,128]{2,1,0:T(1,128)S(1)}, u32[]{:S(2)}) copy-start(f32[16,1,128]{2,1,0:T(1,128)S(1)} %convert_element_type.331) | copy-start | bytes 24580
  86.6 66.5 %copy-start.24 = (f32[256]{0:T(256)}, f32[256]{0:T(256)S(1)}, u32[]{:S(2)}) copy-start(f32[256]{0:T(256)S(1)} %broadcast_multiply_fusion.1) | copy-start | bytes 3076
  88.3 64.8 %copy-start.39 = (f32[256]{0:T(256)}, f32[256]{0:T(256)S(1)}, u32[]{:S(2)}) copy-start(f32[256]{0:T(256)S(1)} %fusion.47) | copy-start | bytes 3076
  88.3 64.8 %copy-start.27 = (f32[256]{0:T(256)}, f32[256]{0:T(256)S(1)}, u32[]{:S(2)}) copy-start(f32[256]{0:T(256)S(1)} %fusion.65) | copy-start | bytes 3076
  153.2 9.4 copy-start.43
  153.2 9.4 copy-start.44
  153.2 29.7 %copy-start.45 = (bf16[128]{0:T(256)(128)(2,1)S(1)}, bf16[128]{0:T(256)(128)(2,1)}, u32[]{:S(2)}) copy-start(bf16[128]{0:T(256)(128)(2,1)} %param.29) | copy-start | bytes 772
  153.2 47.1 %copy-start.46 = (bf16[128]{0:T(256)(128)(2,1)S(1)}, bf16[128]{0:T(256)(128)(2,1)}, u32[]{:S(2)}) copy-start(bf16[128]{0:T(256)(128)(2,1)} %param.30) | copy-start | bytes 772
  157.3 88.2 %all-gather.28.cloned.1.call-start = ((), (), s32[]{:S(2)}) async-start(), calls=%async_computation.17 | async-start | bytes 5242880 | tf_op jit(solution)/shard_map/all_gather | solution.py:77
  160.1 145.9 %all-gather.20.cloned.1.call-start = ((), (), s32[]{:S(2)}) async-start(), calls=%async_computation.7 | async-start | bytes 8912896 | tf_op jit(solution)/shard_map/all_gather | solution.py:62
  160.7 313.2 %all-gather.22.cloned.1.call-start = ((), (), s32[]{:S(2)}) async-start(), calls=%async_computation.8 | async-start | bytes 35651584 | tf_op jit(solution)/shard_map/all_gather | solution.py:104
  161.3 482.1 %all-gather.24.cloned.1.call-start = ((), (), s32[]{:S(2)}) async-start(), calls=%async_computation.9 | async-start | bytes 35651584 | tf_op jit(solution)/shard_map/all_gather | solution.py:106
  161.8 712.1 %reduce-scatter.9.cloned.1.call-start = ((), (), s32[]{:S(2)}) async-start(), calls=%async_computation.11 | async-start | bytes 5242880 | tf_op jit(solution)/shard_map/reduce_scatter | solution.py:193
  200.2 495.1 %copy-start.20 = (f32[16,1,128]{2,1,0:T(1,128)}, f32[16,1,128]{2,1,0:T(1,128)S(1)}, u32[]{:S(2)}) copy-start(f32[16,1,128]{2,1,0:T(1,128)S(1)} %convert_element_type.335) | copy-start | bytes 24580
  219.0 254.8 %copy-start.22 = (f32[16,1,128]{2,1,0:T(1,128)}, f32[16,1,128]{2,1,0:T(1,128)S(1)}, u32[]{:S(2)}) copy-start(f32[16,1,128]{2,1,0:T(1,128)S(1)} %convert_element_type.336) | copy-start | bytes 24580
  238.7 13.2 copy-start.14
  270.5 15.0 copy-start.5
  285.5 20.6 copy-start
  312.2 383.1 %copy-start.3 = (f32[256,2048]{1,0:T(8,128)}, f32[256,2048]{1,0:T(8,128)S(1)}, u32[]{:S(2)}) copy-start(f32[256,2048]{1,0:T(8,128)S(1)} %get-tuple-element.55) | copy-start | bytes 6291460
  312.2 383.1 %copy-start.30 = (f32[256]{0:T(256)}, f32[256]{0:T(256)S(1)}, u32[]{:S(2)}) copy-start(f32[256]{0:T(256)S(1)} %broadcast_multiply_fusion) | copy-start | bytes 3076
  312.6 382.8 %copy-start.32 = (f32[256]{0:T(256)}, f32[256]{0:T(256)S(1)}, u32[]{:S(2)}) copy-start(f32[256]{0:T(256)S(1)} %fusion.66) | copy-start | bytes 3076
  473.8 169.6 %copy-start.10 = (bf16[1,256,2048]{2,1,0:T(8,128)(2,1)S(1)}, bf16[1,256,2048]{2,1,0:T(8,128)(2,1)}, u32[]{:S(2)}) copy-start(bf16[1,256,2048]{2,1,0:T(8,128)(2,1)} %param.31) | copy-start | bytes 3145732
  723.7 150.3 %reduce-scatter.7.cloned.1.call-start = ((), (), s32[]{:S(2)}) async-start(), calls=%async_computation.10 | async-start | bytes 5242880 | tf_op jit(solution)/shard_map/reduce_scatter | solution.py:187
  741.0 61.5 %copy-start.8 = (bf16[32,64,256]{2,1,0:T(8,128)(2,1)S(1)}, bf16[32,64,256]{2,1,0:T(8,128)(2,1)}, u32[]{:S(2)}) copy-start(bf16[32,64,256]{2,1,0:T(8,128)(2,1)} %fusion.54) | copy-start | bytes 3145732
  802.5 227.9 %reduce-scatter.13.cloned.1.call-start = ((), (), s32[]{:S(2)}) async-start(), calls=%async_computation.13 | async-start | bytes 17825792 | tf_op jit(solution)/shard_map/reduce_scatter | solution.py:215
  812.3 61.7 %copy-start.1 = (bf16[1,256,2048]{2,1,0:T(8,128)(2,1)S(1)}, bf16[1,256,2048]{2,1,0:T(8,128)(2,1)}, u32[]{:S(2)}) copy-start(bf16[1,256,2048]{2,1,0:T(8,128)(2,1)} %param.16) | copy-start | bytes 3145732
  812.3 61.7 %copy-start.16 = (f32[16,1,128]{2,1,0:T(1,128)S(1)}, f32[16,1,128]{2,1,0:T(1,128)}, u32[]{:S(2)}) copy-start(f32[16,1,128]{2,1,0:T(1,128)} %copy-done.15) | copy-start | bytes 24580
  812.3 61.7 %copy-start.19 = (f32[16,1,128]{2,1,0:T(1,128)S(1)}, f32[16,1,128]{2,1,0:T(1,128)}, u32[]{:S(2)}) copy-start(f32[16,1,128]{2,1,0:T(1,128)} %copy-done.18) | copy-start | bytes 24580
  812.3 61.7 %copy-start.25 = (f32[256]{0:T(256)S(1)}, f32[256]{0:T(256)}, u32[]{:S(2)}) copy-start(f32[256]{0:T(256)} %copy-done.24) | copy-start | bytes 3076
  812.3 61.7 %copy-start.28 = (f32[256]{0:T(256)S(1)}, f32[256]{0:T(256)}, u32[]{:S(2)}) copy-start(f32[256]{0:T(256)} %copy-done.27) | copy-start | bytes 3076
  812.3 688.9 %reduce-scatter.11.cloned.1.call-start = ((), (), s32[]{:S(2)}) async-start(), calls=%async_computation.12 | async-start | bytes 53477376 | tf_op jit(solution)/shard_map/reduce_scatter | solution.py:212
  874.0 20.8 copy-start.13
  894.8 1246.9 %reduce-scatter.17.cloned.1.call-start = ((), (), s32[]{:S(2)}) async-start(), calls=%async_computation.15 | async-start | bytes 71303168 | tf_op jit(solution)/shard_map/reduce_scatter | solution.py:150
  929.2 1852.5 %reduce-scatter.15.cloned.1.call-start = ((), (), s32[]{:S(2)}) async-start(), calls=%async_computation.14 | async-start | bytes 71303168 | tf_op jit(solution)/shard_map/reduce_scatter | solution.py:148
  956.9 1982.2 %all-reduce.14.cloned.1.call-start = ((), (), s32[]{:S(2)}) async-start(), calls=%async_computation.18 | async-start | bytes 12582912 | tf_op jit(solution)/shard_map/psum | solution.py:221
  2785.5 31.8 %copy-start.36 = (f32[32,64]{1,0:T(8,128)S(1)}, f32[32,64]{1,0:T(8,128)}, u32[]{:S(2)}) copy-start(f32[32,64]{1,0:T(8,128)} %get-tuple-element.58) | copy-start | bytes 24580
  2785.5 33.5 %copy-start.2 = (bf16[1,256,2048]{2,1,0:T(8,128)(2,1)S(1)}, bf16[1,256,2048]{2,1,0:T(8,128)(2,1)}, u32[]{:S(2)}) copy-start(bf16[1,256,2048]{2,1,0:T(8,128)(2,1)} %param.16) | copy-start | bytes 3145732
  2785.6 33.5 %copy-start.17 = (f32[16,1,128]{2,1,0:T(1,128)S(1)}, f32[16,1,128]{2,1,0:T(1,128)}, u32[]{:S(2)}) copy-start(f32[16,1,128]{2,1,0:T(1,128)} %copy-done.15) | copy-start | bytes 24580
  2785.6 33.5 %copy-start.26 = (f32[256]{0:T(256)S(1)}, f32[256]{0:T(256)}, u32[]{:S(2)}) copy-start(f32[256]{0:T(256)} %copy-done.24) | copy-start | bytes 3076
  2819.0 14.8 copy-start.40
  2819.0 14.9 copy-start.29
  2819.1 15.8 copy-start.7
  2819.1 15.8 copy-start.11
  2819.1 15.8 copy-start.38
  2939.1 9.7 copy-start.12
  (14 other events, 38.5 us)
Sparse Core Ops, SparseCore 0:
  9.6 131.3 all-gather.17
  157.4 34.7 all-gather.25
  194.3 34.7 all-gather.27
  231.1 74.8 all-gather.19
  307.5 166.2 all-gather.21
  475.3 168.0 all-gather.23
  723.8 44.4 reduce-scatter.8
  802.6 44.8 reduce-scatter.6
  851.6 178.7 reduce-scatter.12
  1034.5 466.7 reduce-scatter.10
  1505.5 636.1 reduce-scatter.16
  2145.8 635.9 reduce-scatter.14
  2785.7 153.4 all-reduce.13
where the time goes:
time: 2960 us
  waiting for transfers between devices  2190 us (74%)
  matrix products  424 us (14%)
  blocking collectives  238 us (8%)
  other arithmetic  59.3 us (2%)
    reduce_scatter x1, waiting for transfers between devices, shards(): lax.psum_scatter(shrink_term, ('fsdp', 'ctx'), scatter_dimension=0, tiled...  637 us
    reduce_scatter x1, waiting for transfers between devices, shards(): lax.psum_scatter(expand_term, ('fsdp', 'ctx'), scatter_dimension=0, tiled...  636 us
    reduce_scatter x1, waiting for transfers between devices, shards(): lax.psum_scatter(joined_term, ('fsdp', 'ctx'), scatter_dimension=0, tiled...  469 us
    all_gather x1, waiting for transfers between devices, shards(): lax.all_gather(expand_weight, ('fsdp', 'ctx'), axis=0, tiled=True)  161 us
    all_gather x1, waiting for transfers between devices, shards(): lax.all_gather(shrink_weight, ('fsdp', 'ctx'), axis=0, tiled=True)  150 us
    dot_general x1, matrix products, shards(): jnp.einsum('shqk,skhe->sqhe', d_raw, key_heads, preferred_element_type=jn...  61.6 us
    dot_general x1, matrix products, shards(): jnp.einsum('shqk,sqhe->skhe', d_raw, query_heads, preferred_element_type=...  61.5 us
    unnamed x1, blocking collectives  60.8 us
  transfers between devices with their start and end apart: 13, of which 9 were waited for; matrix products, arithmetic and copies ran while one was open for 13% of the time, Pallas kernels for 0%

commit v1 on v0

--- a/solution.py
+++ b/solution.py
@@ -100,10 +100,34 @@
         + jnp.dot(attended, dense_all, preferred_element_type=jnp.float32)
         + dbias_all.astype(jnp.float32)
     )
+
+    def advance_tiles(dim_k, local_x):
+        chip_axis = ("fsdp", "ctx")
+        r_now, latest, n_now = (
+            lax.axis_size(chip_axis),
+            lax.axis_index(chip_axis),
+            local_x.shape[dim_k],
+        )
+        z_new, tall = (local_x, 1)
+        while tall < r_now:
+            z_new = jnp.concatenate(
+                [
+                    z_new,
+                    lax.ppermute(
+                        z_new,
+                        chip_axis,
+                        list(map(lambda kk: (kk, (kk - tall) % r_now), range(r_now))),
+                    ),
+                ],
+                axis=dim_k,
+            )
+            tall = 2 * tall
+        return jnp.roll(z_new, latest * n_now, dim_k)
+
     mlp_parts = (
         lax.all_gather(expand_weight, ("fsdp", "ctx"), axis=0, tiled=True),
         lax.all_gather(expand_bias, ("fsdp", "ctx"), axis=0, tiled=True),
-        lax.all_gather(shrink_weight, ("fsdp", "ctx"), axis=0, tiled=True),
+        advance_tiles(0, shrink_weight),
         lax.all_gather(shrink_bias, ("fsdp", "ctx"), axis=0, tiled=True),
         lax.all_gather(second_gain, ("fsdp", "ctx"), axis=0, tiled=True),
         lax.all_gather(second_shift, ("fsdp", "ctx"), axis=0, tiled=True),

time: 2960 us -> 3700 us (1.25)
  blocking collectives: 238 us -> 620 us
  waiting for transfers between devices: 2190 us -> 2470 us
  local copies, waits for them, and re-layouts: 25.4 us -> 85.5 us
    ppermute x0 -> x4, waiting for transfers between devices: none -> 1040 us  [advance_tiles(): lax.ppermute(z_new, chip_axis, list(map(lambda kk: (kk, (kk - tall) % r_n...]
    reduce_scatter x1, waiting for transfers between devices: 469 us -> 0.01 us  [shards(): lax.psum_scatter(joined_term, ('fsdp', 'ctx'), scatter_dimension=0, tiled...]
    all_gather x1, blocking collectives: 20.2 us -> 403 us  [shards(): lax.all_gather(shrink_bias, ('fsdp', 'ctx'), axis=0, tiled=True)]
    reduce_scatter x1, waiting for transfers between devices: 636 us -> 386 us  [shards(): lax.psum_scatter(expand_term, ('fsdp', 'ctx'), scatter_dimension=0, tiled...]
    reduce_scatter x1, waiting for transfers between devices: 50.7 us -> 0.01 us  [shards(): lax.psum_scatter(dense_term, ('fsdp', 'ctx'), scatter_dimension=0, tiled=...]
    unnamed x109 -> x132, local copies, waits for them, and re-layouts: 7.47 us -> 54.9 us
  transfers between devices with their start and end apart: 13 -> 17, of which waited for: 9 -> 11; matrix products, arithmetic and copies ran while one was open for 13% -> 11% of each run, Pallas kernels for 0% -> 0%
where the time goes in v1:
time: 3700 us
  waiting for transfers between devices  2470 us (67%)
  blocking collectives  620 us (17%)
  matrix products  430 us (12%)
  local copies, waits for them, and re-layouts  85.5 us (2%)
  other arithmetic  72.5 us (2%)
    ppermute x4, waiting for transfers between devices, advance_tiles(): lax.ppermute(z_new, chip_axis, list(map(lambda kk: (kk, (kk - tall) % r_n...  1040 us
    reduce_scatter x1, waiting for transfers between devices, shards(): lax.psum_scatter(shrink_term, ('fsdp', 'ctx'), scatter_dimension=0, tiled...  637 us
    all_gather x1, blocking collectives, shards(): lax.all_gather(shrink_bias, ('fsdp', 'ctx'), axis=0, tiled=True)  403 us
    reduce_scatter x1, waiting for transfers between devices, shards(): lax.psum_scatter(expand_term, ('fsdp', 'ctx'), scatter_dimension=0, tiled...  386 us
    all_gather x1, waiting for transfers between devices, shards(): lax.all_gather(shrink_weight, ('fsdp', 'ctx'), axis=0, tiled=True)  150 us
    all_gather x1, waiting for transfers between devices, shards(): lax.all_gather(expand_weight, ('fsdp', 'ctx'), axis=0, tiled=True)  131 us
    all_gather x1, waiting for transfers between devices, shards(): lax.all_gather(joined_weight, ('fsdp', 'ctx'), axis=0, tiled=True)  88.6 us
  transfers between devices with their start and end apart: 17, of which 11 were waited for; matrix products, arithmetic and copies ran while one was open for 11% of the time, Pallas kernels for 0%

profile of v1, /device:TPU:0, one launch (start us, length us, event | category | flops | bytes accessed | tf_op | source)
XLA Modules:
  0.0 3698.7 jit_solution(6269643087195217235)
XLA Ops:
  8.0 23.2 all-gather.2
  31.2 17.5 all-gather.3
  52.4 88.6 %all-gather.18.cloned.1.call-done = bf16[2048,6144]{1,0:T(8,128)(2,1)} async-done(((bf16[128,6144]{1,0:T(8,128)(2,1)}), bf16[2048,6144]{1,0:T(8,128)(2,1)}) %all-gather.18.cloned.1.call-update) | async-done | bytes 25165840 | tf_op jit(solution)/shard_map/all_gather | solution.py:59
  141.0 12.1 fusion.88
  157.0 20.3 all-gather.5
  177.4 17.3 all-gather.4
  200.8 18.7 all-gather.6
  219.6 17.3 all-gather.7
  236.9 18.9 all-gather.8
  255.9 17.9 all-gather.9
  274.9 6.8 copy.45
  281.7 6.4 copy.43
  288.1 18.0 select_reduce_fusion
  306.1 15.9 fusion.4
  322.0 15.5 fusion.63
  337.5 6.4 fusion.95
  345.2 131.1 %all-gather.22.cloned.1.call-done = bf16[2048,8192]{1,0:T(8,128)(2,1)} async-done(((bf16[128,8192]{1,0:T(8,128)(2,1)}), bf16[2048,8192]{1,0:T(8,128)(2,1)}) %all-gather.22.cloned.1.call-update) | async-done | bytes 33554448 | tf_op jit(solution)/shard_map/all_gather | solution.py:128
  476.4 20.0 convolution_add_fusion
  496.4 149.5 %all-gather.24.cloned.1.call-done = bf16[8192,2048]{1,0:T(8,128)(2,1)} async-done(((bf16[512,2048]{1,0:T(8,128)(2,1)}), bf16[8192,2048]{1,0:T(8,128)(2,1)}) %all-gather.24.cloned.1.call-update) | async-done | bytes 33554448 | tf_op jit(solution)/shard_map/all_gather | solution.py:150
  645.9 33.5 convert_reduce_fusion
  679.5 18.6 multiply_reduce_fusion.1
  703.6 6.7 convolution_convert_fusion
  711.8 15.3 fusion.98
  727.2 60.9 %fusion.29 = bf16[32,64,1024]{2,1,0:T(8,128)(2,1)} fusion(bf16[256,32,64]{0,2,1:T(8,128)(2,1)} %bitcast.140, f32[32,256,1024]{2,1,0:T(8,128)} %fusion.98, f32[32,256,1024]{2,1,0:T(8,128)} %get-tuple-element.53, f32[32,256]{1,0:T(8,128)S(1)} %copy-done.35, pred[256,1024]{1,0:T(8,128)(4,1)S(1)} %copy-done.21), kind=kOutput, calls=%fused_computation.48 | convolution fusion | flops 1151345664 | bytes 72646656 | tf_op jit(solution)/shard_map/shqk,sqhe->skhe/dot_general | solution.py:204
  788.1 17.4 fusion.32
  805.6 10.0 fusion.99
  815.8 61.3 %convert_reduce_fusion.5 = (f32[32,64]{1,0:T(8,128)}, bf16[32,64,256]{2,1,0:T(8,128)(2,1)}) fusion(bf16[1024,32,64]{0,2,1:T(8,128)(2,1)} %bitcast.133, f32[32,256,1024]{2,1,0:T(8,128)} %fusion.98, f32[32,256,1024]{2,1,0:T(8,128)} %get-tuple-element.53, f32[32,256]{1,0:T(8,128)S(1)} %copy-done.35, pred[256,1024]{1,0:T(8,128)(4,1)S(1)} %copy-done.21), kind=kOutput, calls=%fused_computation.80 | convolution fusion | flops 1150819328 | bytes 72654848 | tf_op jit(solution)/shard_map/shqk,skhe->sqhe/dot_general | solution.py:203
  880.7 26.0 fusion.65
  907.4 27.1 fusion.91
  935.7 34.3 fusion.67
  973.6 38.3 %collective-permute-done = bf16[512,2048]{1,0:T(8,128)(2,1)S(1)} collective-permute-done((bf16[512,2048]{1,0:T(8,128)(2,1)S(1)}, bf16[512,2048]{1,0:T(8,128)(2,1)S(1)}, u32[]{:S(2)}, u32[]{:S(2)}) %collective-permute-start) | collective-permute-done | bytes 2097184 | tf_op jit(solution)/shard_map/ppermute | solution.py:116
  1012.6 93.4 %collective-permute-done.1 = bf16[1024,2048]{1,0:T(8,128)(2,1)S(1)} collective-permute-done((bf16[1024,2048]{1,0:T(8,128)(2,1)S(1)}, bf16[1024,2048]{1,0:T(8,128)(2,1)S(1)}, u32[]{:S(2)}, u32[]{:S(2)}) %collective-permute-start.1) | collective-permute-done | bytes 4194336 | tf_op jit(solution)/shard_map/ppermute | solution.py:116
  1110.2 284.3 %collective-permute-done.2 = bf16[2048,2048]{1,0:T(8,128)(2,1)S(1)} collective-permute-done((bf16[2048,2048]{1,0:T(8,128)(2,1)S(1)}, bf16[2048,2048]{1,0:T(8,128)(2,1)S(1)}, u32[]{:S(2)}, u32[]{:S(2)}) %collective-permute-start.2) | collective-permute-done | bytes 8388640 | tf_op jit(solution)/shard_map/ppermute | solution.py:116
  1394.5 8.9 pad_maximum_fusion
  1405.3 403.5 %all-gather.10 = bf16[16,1,128]{2,1,0:T(2,128)(2,1)S(1)} all-gather(bf16[1,1,128]{2,1,0:T(2,128)(2,1)S(1)} %bitcast.166), channel_id=1, replica_groups=mesh['rep'=2,'fsdp'=4,'ctx'=4] {'fsdp','ctx'}, dimensions={0}, use_global_device_ids=true | all-gather | bytes 4352 | tf_op jit(solution)/shard_map/all_gather | solution.py:131
  1816.3 8.3 constant_dynamic-update-slice_fusion.6
  1824.6 623.4 %collective-permute-done.3 = bf16[4096,2048]{1,0:T(8,128)(2,1)} collective-permute-done((bf16[4096,2048]{1,0:T(8,128)(2,1)}, bf16[4096,2048]{1,0:T(8,128)(2,1)}, u32[]{:S(2)}, u32[]{:S(2)}) %collective-permute-start.3) | collective-permute-done | bytes 16777248 | tf_op jit(solution)/shard_map/ppermute | solution.py:116
  2448.0 14.4 constant_dynamic-update-slice_fusion.5
  2468.4 8.4 constant_dynamic-update-slice_fusion.1
  2476.8 14.3 constant_dynamic-update-slice_fusion
  2496.5 386.3 %reduce-scatter.15.cloned.1.call-done = f32[128,8192]{1,0:T(8,128)} async-done(((f32[2048,8192]{1,0:T(8,128)}), f32[128,8192]{1,0:T(8,128)}) %reduce-scatter.15.cloned.1.call-update) | async-done | bytes 4194320 | tf_op jit(solution)/shard_map/reduce_scatter | solution.py:172
  2886.6 636.5 %reduce-scatter.17.cloned.1.call-done = f32[512,2048]{1,0:T(8,128)} async-done(((f32[8192,2048]{1,0:T(8,128)}), f32[512,2048]{1,0:T(8,128)}) %reduce-scatter.17.cloned.1.call-update) | async-done | bytes 4194320 | tf_op jit(solution)/shard_map/reduce_scatter | solution.py:174
  3527.0 31.6 fusion.48
  3560.3 15.1 fusion.92
  3578.9 60.7 %all-reduce.9 = (bf16[2048]{0:T(1024)(128)(2,1)S(1)}, bf16[2048]{0:T(1024)(128)(2,1)S(1)}, bf16[2048]{0:T(1024)(128)(2,1)S(1)}, bf16[8192]{0:T(1024)(128)(2,1)S(...) all-reduce(f32[2048]{0:T(1024)S(1)} %reduce_sum.189, ...), channel_id=7, replica_groups=mesh['rep'=2,'fsdp'=4,'ctx'=4] {'fsdp','ctx'}, use_global_device_ids=true, to_apply=%region_16.17.clone | all-reduce | flops 24576 | bytes 147456
  3640.3 5.1 all-reduce.10
  3650.1 30.5 all-reduce.14.cloned.1.call-done
  3680.6 4.2 convert_element_type.314
  (220 shorter events, 82.0 us)
Async XLA Ops:
  7.2 133.8 %all-gather.18.cloned.1.call-start = ((), (), s32[]{:S(2)}) async-start(), calls=%async_computation.6 | async-start | bytes 26738688 | tf_op jit(solution)/shard_map/all_gather | solution.py:59
  7.9 267.0 %all-gather.28.cloned.1.call-start = ((), (), s32[]{:S(2)}) async-start(), calls=%async_computation.17 | async-start | bytes 5242880 | tf_op jit(solution)/shard_map/all_gather | solution.py:77
  31.2 121.9 %copy-start.24 = (f32[16,1,128]{2,1,0:T(1,128)}, f32[16,1,128]{2,1,0:T(1,128)S(1)}, u32[]{:S(2)}) copy-start(f32[16,1,128]{2,1,0:T(1,128)S(1)} %convert_element_type.330) | copy-start | bytes 24580
  48.7 104.4 %copy-start.27 = (f32[16,1,128]{2,1,0:T(1,128)}, f32[16,1,128]{2,1,0:T(1,128)S(1)}, u32[]{:S(2)}) copy-start(f32[16,1,128]{2,1,0:T(1,128)S(1)} %convert_element_type.331) | copy-start | bytes 24580
  50.2 102.9 %copy-start.32 = (f32[256]{0:T(256)}, f32[256]{0:T(256)S(1)}, u32[]{:S(2)}) copy-start(f32[256]{0:T(256)S(1)} %broadcast_multiply_fusion.1) | copy-start | bytes 3076
  52.4 100.8 %copy-start.36 = (f32[256]{0:T(256)}, f32[256]{0:T(256)S(1)}, u32[]{:S(2)}) copy-start(f32[256]{0:T(256)S(1)} %fusion.74) | copy-start | bytes 3076
  141.0 36.4 copy-start.50
  155.8 45.1 %copy-start.51 = (bf16[128]{0:T(256)(128)(2,1)S(1)}, bf16[128]{0:T(256)(128)(2,1)}, u32[]{:S(2)}) copy-start(bf16[128]{0:T(256)(128)(2,1)} %param.22) | copy-start | bytes 772
  155.8 63.8 %copy-start.52 = (bf16[128]{0:T(256)(128)(2,1)S(1)}, bf16[128]{0:T(256)(128)(2,1)}, u32[]{:S(2)}) copy-start(bf16[128]{0:T(256)(128)(2,1)} %param.29) | copy-start | bytes 772
  155.8 81.1 %copy-start.53 = (bf16[128]{0:T(256)(128)(2,1)S(1)}, bf16[128]{0:T(256)(128)(2,1)}, u32[]{:S(2)}) copy-start(bf16[128]{0:T(256)(128)(2,1)} %param.30) | copy-start | bytes 772
  155.8 100.1 %copy-start.48 = (bf16[512]{0:T(512)(128)(2,1)S(1)}, bf16[512]{0:T(512)(128)(2,1)}, u32[]{:S(2)}) copy-start(bf16[512]{0:T(512)(128)(2,1)} %param.24) | copy-start | bytes 3076
  156.9 124.7 %all-gather.26.cloned.1.call-start = ((), (), s32[]{:S(2)}) async-start(), calls=%async_computation.16 | async-start | bytes 5242880 | tf_op jit(solution)/shard_map/all_gather | solution.py:78
  198.4 139.2 %all-gather.20.cloned.1.call-start = ((), (), s32[]{:S(2)}) async-start(), calls=%async_computation.7 | async-start | bytes 8912896 | tf_op jit(solution)/shard_map/all_gather | solution.py:62
  199.0 277.4 %all-gather.22.cloned.1.call-start = ((), (), s32[]{:S(2)}) async-start(), calls=%async_computation.8 | async-start | bytes 35651584 | tf_op jit(solution)/shard_map/all_gather | solution.py:128
  199.6 446.3 %all-gather.24.cloned.1.call-start = ((), (), s32[]{:S(2)}) async-start(), calls=%async_computation.9 | async-start | bytes 35651584 | tf_op jit(solution)/shard_map/all_gather | solution.py:150
  200.1 676.9 %reduce-scatter.7.cloned.1.call-start = ((), (), s32[]{:S(2)}) async-start(), calls=%async_computation.10 | async-start | bytes 5242880 | tf_op jit(solution)/shard_map/reduce_scatter | solution.py:211
  255.9 220.5 %copy-start.30 = (f32[16,1,128]{2,1,0:T(1,128)}, f32[16,1,128]{2,1,0:T(1,128)S(1)}, u32[]{:S(2)}) copy-start(f32[16,1,128]{2,1,0:T(1,128)S(1)} %convert_element_type.336) | copy-start | bytes 24580
  274.1 47.9 %copy-start.20 = (pred[256,1024]{1,0:T(8,128)(4,1)}, pred[256,1024]{1,0:T(8,128)(4,1)S(1)}, u32[]{:S(2)}) copy-start(pred[256,1024]{1,0:T(8,128)(4,1)S(1)} %fusion.73) | copy-start | bytes 786436
  343.9 562.8 %copy-start.10 = (f32[256,2048]{1,0:T(8,128)}, f32[256,2048]{1,0:T(8,128)S(1)}, u32[]{:S(2)}) copy-start(f32[256,2048]{1,0:T(8,128)S(1)} %get-tuple-element.55) | copy-start | bytes 6291460
  476.4 169.6 %copy-start.17 = (bf16[1,256,2048]{2,1,0:T(8,128)(2,1)S(1)}, bf16[1,256,2048]{2,1,0:T(8,128)(2,1)}, u32[]{:S(2)}) copy-start(bf16[1,256,2048]{2,1,0:T(8,128)(2,1)} %param.31) | copy-start | bytes 3145732
  788.1 92.6 %reduce-scatter.9.cloned.1.call-start = ((), (), s32[]{:S(2)}) async-start(), calls=%async_computation.11 | async-start | bytes 5242880 | tf_op jit(solution)/shard_map/reduce_scatter | solution.py:217
  805.6 1685.6 %reduce-scatter.13.cloned.1.call-start = ((), (), s32[]{:S(2)}) async-start(), calls=%async_computation.13 | async-start | bytes 17825792 | tf_op jit(solution)/shard_map/reduce_scatter | solution.py:239
  815.7 65.0 %copy-start.8 = (bf16[1,256,2048]{2,1,0:T(8,128)(2,1)S(1)}, bf16[1,256,2048]{2,1,0:T(8,128)(2,1)}, u32[]{:S(2)}) copy-start(bf16[1,256,2048]{2,1,0:T(8,128)(2,1)} %param.16) | copy-start | bytes 3145732
  815.7 65.0 %copy-start.25 = (f32[16,1,128]{2,1,0:T(1,128)S(1)}, f32[16,1,128]{2,1,0:T(1,128)}, u32[]{:S(2)}) copy-start(f32[16,1,128]{2,1,0:T(1,128)} %copy-done.24) | copy-start | bytes 24580
  815.7 65.0 %copy-start.28 = (f32[16,1,128]{2,1,0:T(1,128)S(1)}, f32[16,1,128]{2,1,0:T(1,128)}, u32[]{:S(2)}) copy-start(f32[16,1,128]{2,1,0:T(1,128)} %copy-done.27) | copy-start | bytes 24580
  815.7 65.0 %copy-start.33 = (f32[256]{0:T(256)S(1)}, f32[256]{0:T(256)}, u32[]{:S(2)}) copy-start(f32[256]{0:T(256)} %copy-done.32) | copy-start | bytes 3076
  815.7 64.9 %copy-start.37 = (f32[256]{0:T(256)S(1)}, f32[256]{0:T(256)}, u32[]{:S(2)}) copy-start(f32[256]{0:T(256)} %copy-done.36) | copy-start | bytes 3076
  815.7 1677.5 %reduce-scatter.11.cloned.1.call-start = ((), (), s32[]{:S(2)}) async-start(), calls=%async_computation.12 | async-start | bytes 53477376 | tf_op jit(solution)/shard_map/reduce_scatter | solution.py:236
  906.7 1976.1 %reduce-scatter.15.cloned.1.call-start = ((), (), s32[]{:S(2)}) async-start(), calls=%async_computation.14 | async-start | bytes 71303168 | tf_op jit(solution)/shard_map/reduce_scatter | solution.py:172
  934.5 2588.7 %reduce-scatter.17.cloned.1.call-start = ((), (), s32[]{:S(2)}) async-start(), calls=%async_computation.15 | async-start | bytes 71303168 | tf_op jit(solution)/shard_map/reduce_scatter | solution.py:174
  970.1 2710.5 %all-reduce.14.cloned.1.call-start = ((), (), s32[]{:S(2)}) async-start(), calls=%async_computation.18 | async-start | bytes 12582912 | tf_op jit(solution)/shard_map/psum | solution.py:245
  971.6 40.4 %collective-permute-start = (bf16[512,2048]{1,0:T(8,128)(2,1)S(1)}, bf16[512,2048]{1,0:T(8,128)(2,1)S(1)}, u32[]{:S(2)}, u32[]{:S(2)}) collective-permute-start(bf16[512,2048]{1,0:T(8,128)(2,1)S(1)} %copy-done.1), channel_id=1, source_target_pairs={{0,15},{1,0},{2,1},{3,2},{4,3},{5,4},{6,5},{7,6},{8,7},{9,8},{10,9... | collective-permute-start | bytes 6291464 | tf_op jit(solution)/shard_map/ppermute | solution.py:116
  1012.0 382.5 %copy-start.5 = (bf16[512,2048]{1,0:T(8,128)(2,1)}, bf16[512,2048]{1,0:T(8,128)(2,1)S(1)}, u32[]{:S(2)}) copy-start(bf16[512,2048]{1,0:T(8,128)(2,1)S(1)} %collective-permute-done) | copy-start | bytes 6291460
  1012.5 93.5 %collective-permute-start.1 = (bf16[1024,2048]{1,0:T(8,128)(2,1)S(1)}, bf16[1024,2048]{1,0:T(8,128)(2,1)S(1)}, u32[]{:S(2)}, u32[]{:S(2)}) collective-permute-start(bf16[1024,2048]{1,0:T(8,128)(2,1)S(1)} %pad_maximum_fusion.2), channel_id=1, source_target_pairs={{0,14},{1,15},{2,0},{3,1},{4,2},{5,3},{6,4},{7,5},{8,6},{9,7},{10,... | collective-permute-start | bytes 12582920 | tf_op jit(solution)/shard_map/ppermute | solution.py:116
  1106.0 288.4 %copy-start.2 = (bf16[1024,2048]{1,0:T(8,128)(2,1)}, bf16[1024,2048]{1,0:T(8,128)(2,1)S(1)}, u32[]{:S(2)}) copy-start(bf16[1024,2048]{1,0:T(8,128)(2,1)S(1)} %collective-permute-done.1) | copy-start | bytes 12582916
  1107.3 296.1 %copy-start.55 = (u32[32]{0:T(128)S(1)}, u32[32]{0:T(128)}, u32[]{:S(2)}) copy-start(u32[32]{0:T(128)} %constant.131) | copy-start | bytes 388
  1107.3 298.0 %copy-start.54 = (bf16[128]{0:T(256)(128)(2,1)S(1)}, bf16[128]{0:T(256)(128)(2,1)}, u32[]{:S(2)}) copy-start(bf16[128]{0:T(256)(128)(2,1)} %param.26) | copy-start | bytes 772
  1107.3 287.1 %collective-permute-start.2 = (bf16[2048,2048]{1,0:T(8,128)(2,1)S(1)}, bf16[2048,2048]{1,0:T(8,128)(2,1)S(1)}, u32[]{:S(2)}, u32[]{:S(2)}) collective-permute-start(bf16[2048,2048]{1,0:T(8,128)(2,1)S(1)} %pad_maximum_fusion.1), channel_id=1, source_target_pairs={{0,12},{1,13},{2,14},{3,15},{4,0},{5,1},{6,2},{7,3},{8,4},{9,5},{1... | collective-permute-start | bytes 25165832 | tf_op jit(solution)/shard_map/ppermute | solution.py:116
  1403.4 1044.6 %collective-permute-start.3 = (bf16[4096,2048]{1,0:T(8,128)(2,1)}, bf16[4096,2048]{1,0:T(8,128)(2,1)}, u32[]{:S(2)}, u32[]{:S(2)}) collective-permute-start(bf16[4096,2048]{1,0:T(8,128)(2,1)} %pad_maximum_fusion), channel_id=1, source_target_pairs={{0,8},{1,9},{2,10},{3,11},{4,12},{5,13},{6,14},{7,15},{8,0},{9,1},... | collective-permute-start | bytes 50331656 | tf_op jit(solution)/shard_map/ppermute | solution.py:116
  1824.6 639.2 %copy-start.6 = (bf16[512,2048]{1,0:T(8,128)(2,1)S(1)}, bf16[512,2048]{1,0:T(8,128)(2,1)}, u32[]{:S(2)}) copy-start(bf16[512,2048]{1,0:T(8,128)(2,1)} %copy-done.5) | copy-start | bytes 6291460
  2496.5 1030.5 %copy-start.11 = (f32[256,2048]{1,0:T(8,128)S(1)}, f32[256,2048]{1,0:T(8,128)}, u32[]{:S(2)}) copy-start(f32[256,2048]{1,0:T(8,128)} %copy-done.10) | copy-start | bytes 6291460
  3527.0 31.6 copy-start.41
  3527.0 33.2 copy-start.9
  3527.0 33.2 copy-start.26
  3527.0 33.2 copy-start.34
  3560.3 16.1 copy-start.14
  3560.3 16.1 copy-start.19
  3560.3 16.1 copy-start.43
  (25 other events, 191.2 us)
Sparse Core Ops, SparseCore 0:
  9.6 131.3 all-gather.17
  157.1 34.6 all-gather.27
  198.5 32.9 all-gather.25
  233.5 74.9 all-gather.19
  310.0 166.3 all-gather.21
  477.8 168.0 all-gather.23
  788.2 44.5 reduce-scatter.6
  836.0 44.5 reduce-scatter.8
  884.8 319.9 reduce-scatter.12
  1208.8 984.5 reduce-scatter.10
  2197.7 685.1 reduce-scatter.14
  2886.9 636.1 reduce-scatter.16
  3527.1 153.4 all-reduce.13
